TPU v7x, 256 devices: a whole 4x4x8 slice. The times are simulated.
256 devices in a mesh: py: 8 (over z_lo, core), px: 32 (over y, z_hi, x).
Axes of the slice: x: 4, y: 4, z: 8 (z_hi: 2, z_lo: 4; z = z_hi * 4 + z_lo), core: 2. Of those that a mesh axis runs over, the one named last changes fastest.
Arguments:
- measured: float32 [2, 2, 8, 32, 12544], P(None, None, 'py', 'px'), may hold values from -250 to 250
- psf_taps: bfloat16 [8, 32, 32, 32, 32], P('py', 'px'), may hold values from 0 to 0.011047363
- offsets: int32 [8, 32, 2], P('py', 'px'), may hold values from 0 to 7
- window_mask: int32 [1024, 4096], P('py', 'px'), may hold values 0 or 1
Outputs:
- object_basis: float32 [2, 2, 8, 32, 12544], P(None, None, 'py', 'px')
- image_basis: float32 [2, 2, 8, 32, 12544], P(None, None, 'py', 'px')
- factors: float32 [3, 2, 2], replicated
All inputs are finite; a program needn't handle non-finite values. No bound on the sum of `window_mask` on one device may be relied on, other than what follows from the above.
Results may differ from a plain program's by a relative error of at most 0.014.
Values may be sent and summed in bfloat16 or wider, within the bound.
A program may use at most 128 MiB of HBM per device.

v0:
```python
import math

import jax
import jax.numpy as jnp
from jax import lax
from jax.sharding import PartitionSpec as P

PLANES = 2
PATCH = 128
KERNEL = 32
DEPTH_LEN = 64
HALF = 8
CORE = 112


epsilon = 1e-06


def padded_2(shard, sides, width):
    for axis, dim in sides:
        size, length = (lax.axis_size(axis), shard.shape[dim])
        up = [(i, (i + 1) % size) for i in range(size - 1)]
        down = [(j, i) for i, j in up]
        last = lax.slice_in_dim(shard, length - width, length, axis=dim)
        leading = lax.slice_in_dim(shard, 0, width, axis=dim)
        before = lax.ppermute(last, axis, up)
        after = lax.ppermute(leading, axis, down)
        shard = jnp.concatenate([before, shard, after], axis=dim)
    return shard


def twiddle(rows, cols, length, shift):
    row_ids = jnp.arange(rows, dtype=jnp.int32)[:, None]
    col_ids = jnp.arange(cols, dtype=jnp.int32)[None, :] + jnp.asarray(shift).astype(jnp.int32)
    phase = row_ids * col_ids % length
    angle = phase.astype(jnp.float32) * jnp.float32(2.0 * math.pi / length)
    return (jnp.cos(angle).astype(jnp.bfloat16), (-jnp.sin(angle)).astype(jnp.bfloat16))


def product(form, table, values):
    return jnp.einsum(form, table, values, preferred_element_type=jnp.float32)


def complex_axis(form, cos_table, sin_table, real_in, imag_in):
    real_out = product(form, cos_table, real_in) - product(form, sin_table, imag_in)
    imag_out = product(form, cos_table, imag_in) + product(form, sin_table, real_in)
    return (real_out.astype(jnp.bfloat16), imag_out.astype(jnp.bfloat16))


def spectrum(patch_taps, shift_rows, shift_cols):
    half_kernel = KERNEL // 2
    cos_x, sin_x = twiddle(PATCH, KERNEL, PATCH, shift_cols - half_kernel)
    real_x = product("fi,tji->tjf", cos_x, patch_taps).astype(jnp.bfloat16)
    imag_x = product("fi,tji->tjf", sin_x, patch_taps).astype(jnp.bfloat16)
    cos_y, sin_y = twiddle(PATCH, KERNEL, PATCH, shift_rows - half_kernel)
    real_y, imag_y = complex_axis("gj,tjf->tgf", cos_y, sin_y, real_x, imag_x)
    cos_z, sin_z = twiddle(DEPTH_LEN, KERNEL, DEPTH_LEN, -half_kernel)
    return complex_axis("qt,tgf->qgf", cos_z, sin_z, real_y, imag_y)


def blur(patch_cells, spec_real, spec_imag, adjoint):
    values = patch_cells.astype(jnp.bfloat16)
    cos_p, sin_p = twiddle(PATCH, PATCH, PATCH, 0)
    real_x = product("fx,bzyx->bzyf", cos_p, values).astype(jnp.bfloat16)
    imag_x = product("fx,bzyx->bzyf", sin_p, values).astype(jnp.bfloat16)
    real_y, imag_y = complex_axis("gy,bzyf->bzgf", cos_p, sin_p, real_x, imag_x)
    cos_z, sin_z = twiddle(DEPTH_LEN, PLANES, DEPTH_LEN, 0)
    depth_re, depth_im = complex_axis("qz,bzgf->bqgf", cos_z, sin_z, real_y, imag_y)
    kernel_re = spec_real.astype(jnp.float32)
    kernel_im = spec_imag.astype(jnp.float32)
    if adjoint:
        kernel_im = -kernel_im
    depth_re = depth_re.astype(jnp.float32)
    depth_im = depth_im.astype(jnp.float32)
    prod_re = (depth_re * kernel_re - depth_im * kernel_im).astype(jnp.bfloat16)
    prod_im = (depth_re * kernel_im + depth_im * kernel_re).astype(jnp.bfloat16)
    back_cos, back_sin = twiddle(PLANES, DEPTH_LEN, DEPTH_LEN, 0)
    plane_re, plane_im = complex_axis("zq,bqgf->bzgf", back_cos, -back_sin, prod_re, prod_im)
    row_re, row_im = complex_axis("yg,bzgf->bzyf", cos_p, -sin_p, plane_re, plane_im)
    spatial = product("xf,bzyf->bzyx", cos_p, row_re) + product("xf,bzyf->bzyx", sin_p, row_im)
    return spatial * jnp.float32(1.0 / (DEPTH_LEN * PATCH * PATCH))


def window(mask_block):
    return mask_block.astype(jnp.float32)


def fold_owned(padded, dim):
    lower = lax.slice_in_dim(padded, 0, HALF, axis=dim) + lax.slice_in_dim(
        padded, 2 * HALF, 3 * HALF, axis=dim
    )
    middle = lax.slice_in_dim(padded, 3 * HALF, PATCH - HALF, axis=dim)
    upper = lax.slice_in_dim(padded, PATCH - HALF, PATCH, axis=dim) + lax.slice_in_dim(
        padded, PATCH + HALF, PATCH + 2 * HALF, axis=dim
    )
    return jnp.concatenate([lower, middle, upper], axis=dim)


def gram_terms(pair):
    return (jnp.sum(pair[0] * pair[0]), jnp.sum(pair[0] * pair[1]), jnp.sum(pair[1] * pair[1]))


def factor(terms, count):
    r_first = jnp.sqrt(terms[0] / count + epsilon)
    r_cross = terms[1] / count / r_first
    r_second = jnp.sqrt(terms[2] / count - r_cross * r_cross + epsilon)
    return (r_first, r_cross, r_second)


def solve_right(pair, triple):
    leading = pair[0] / triple[0]
    trailing = (pair[1] - triple[1] * leading) / triple[2]
    return jnp.stack([leading, trailing])


def packed(triple):
    return jnp.stack(
        [jnp.stack([triple[0], triple[1]]), jnp.stack([jnp.zeros_like(triple[0]), triple[2]])]
    )


def flatten_cells(block):
    return block.reshape(2, PLANES, 1, 1, CORE * CORE)


def body(measured, psf_taps, offsets, window_mask):
    count_rows = lax.axis_size("py")
    count_cols = lax.axis_size("px")
    count = jnp.float32(PLANES * CORE * CORE * count_rows * count_cols)
    spec_real, spec_imag = spectrum(psf_taps[0, 0], offsets[0, 0, 0], offsets[0, 0, 1])
    weight = window(window_mask)
    first_sq, first_cross, first_tail = gram_terms(measured)
    start_terms = lax.psum((first_sq, first_cross, first_tail), ("py", "px"))
    start_factor = factor(start_terms, count)
    left_flat = solve_right(measured, start_factor)
    left_basis = left_flat.reshape(2, PLANES, CORE, CORE)
    left_narrow = left_basis.astype(jnp.bfloat16)
    left_patch = padded_2(left_narrow, (("py", 2), ("px", 3)), HALF)
    adjoint_patch = blur(left_patch, spec_real, spec_imag, True) * weight
    folded = padded_2(adjoint_patch, (("py", 2), ("px", 3)), HALF)
    adjoint_core = fold_owned(fold_owned(folded, 2), 3)
    second_sq, second_cross, second_tail = gram_terms(adjoint_core)
    alpha_terms = lax.psum((second_sq, second_cross, second_tail), ("py", "px"))
    alpha_factor = factor(alpha_terms, count)
    object_basis = solve_right(adjoint_core, alpha_factor)
    object_patch = padded_2(object_basis, (("py", 2), ("px", 3)), HALF)
    forward_patch = blur(object_patch * weight, spec_real, spec_imag, False)
    forward_padded = padded_2(forward_patch, (("py", 2), ("px", 3)), HALF)
    forward_core = fold_owned(fold_owned(forward_padded, 2), 3)
    residue = jnp.stack(
        [
            forward_core[0] - alpha_factor[0] * left_basis[0] - alpha_factor[1] * left_basis[1],
            forward_core[1] - alpha_factor[2] * left_basis[1],
        ]
    )
    third_sq, third_cross, third_tail = gram_terms(residue)
    beta_terms = lax.psum((third_sq, third_cross, third_tail), ("py", "px"))
    beta_factor = factor(beta_terms, count)
    image_basis = solve_right(residue, beta_factor)
    factors = jnp.stack([packed(start_factor), packed(alpha_factor), packed(beta_factor)])
    return (flatten_cells(object_basis), flatten_cells(image_basis), factors)


def solution(mesh):
    placed = (
        P(None, None, "py", "px", None),
        P("py", "px", None, None, None),
        P("py", "px", None),
        P("py", "px"),
    )
    return jax.shard_map(
        body,
        mesh=mesh,
        in_specs=placed,
        out_specs=(P(None, None, "py", "px", None), P(None, None, "py", "px", None), P()),
        check_vma=False,
    )
```

profile of v0, /device:TPU:1, one launch (start us, length us, event | category | flops | bytes accessed | tf_op | source)
XLA Modules:
  0.0 463.5 jit_solution(16604225201026241020)
XLA Ops:
  0.6 1.8 multiply_reduce_fusion.10
  2.5 81.5 %all-reduce.2 = (f32[]{:T(128)}, f32[]{:T(128)}, f32[]{:T(128)}) all-reduce(f32[]{:T(128)} %get-tuple-element.14, f32[]{:T(128)} %get-tuple-element.13, f32[]{:T(128)} %get-tuple-element.12), channel_id=1, replica_groups=mesh['py'=8,'px'=32] {'py','px'}, use_global_device_ids=true, to_apply=%region_1.2 | all-reduce | flops 3 | bytes 24 | tf_op jit(solution)/shard_map/psum | solution.py:133
  86.1 1.8 convert_reduce_fusion.1
  88.6 2.8 collective-permute-start.1
  91.4 2.7 collective-permute-start
  94.2 1.3 fusion.386
  98.7 1.6 fusion.11
  100.2 1.9 copy.14
  102.2 1.6 fusion.10
  103.7 1.9 copy.13
  106.5 0.9 fusion.136
  107.4 4.1 fusion.387
  111.5 2.9 fusion.8
  114.6 1.3 collective-permute-start.3
  115.9 14.7 %collective-permute-start.2 = (bf16[2,2,128,8]{3,2,1,0:T(8,128)(2,1)S(1)}, bf16[2,2,128,8]{3,2,1,0:T(8,128)(2,1)S(1)}, u32[]{:S(2)}, u32[]{:S(2)}) collective-permute-start(bf16[2,2,128,8]{3,2,1,0:T(8,128)(2,1)S(1)} %get-tuple-element.53), channel_id=1, source_target_pairs={{0,1},{1,2},{2,3},{3,4},{4,5},{5,6},{6,7},{7,8},{8,9},{9,10},{10,1... | collective-permute-start | bytes 24584 | tf_op jit(solution)/shard_map/ppermute | solution.py:26
  133.0 4.6 fusion.177
  138.2 5.4 %fusion.175 = f32[2,128,128,64]{2,3,1,0:T(8,128)} fusion(bf16[2,2,128,128]{3,1,2,0:T(2,128)(2,1)S(1)} %copy.12), kind=kOutput, calls=%fused_computation.253 | convolution fusion | flops 8390528 | bytes 8519680 | tf_op jit(solution)/shard_map/qz,bzgf->bqgf/dot_general | solution.py:41
  144.1 3.5 subtract_convert_fusion.1
  147.6 1.5 copy-done.7
  149.1 7.4 %fusion.7 = (bf16[2,64,128,128]{3,1,2,0:T(8,128)(2,1)S(1)}, bf16[2,64,128,128]{3,1,2,0:T(8,128)(2,1)S(1)}) fusion(bf16[2,128,128,64]{2,3,1,0:T(8,128)(2,1)} %subtract_convert_fusion.1, f32[64,128,128]{2,0,1:T(8,128)S(1)} %copy-done.7, f32[64,128,128]{2,0,1:T(8,128)S(1)} %copy-done.2, f32[2,128,128,64]{2,3,1,0:T(8,128)} %fusion.175, ...), kind=kOutput, calls=%fused_computation.13 | convolution fusion | flops 33556480 | bytes 29491200 | tf_op jit(solution)/shard_map/qz,bzgf->bqgf/dot_general | solution.py:41
  159.7 2.9 fusion.38
  164.2 2.2 collective-permute-start.5
  166.4 3.4 collective-permute-start.4
  170.8 1.3 collective-permute-start.7
  172.1 4.0 collective-permute-start.6
  176.2 4.7 %collective-permute-done.7 = f32[2,2,144,8]{3,2,1,0:T(8,128)S(1)} collective-permute-done((f32[2,2,144,8]{3,2,1,0:T(8,128)S(1)}, f32[2,2,144,8]{3,2,1,0:T(8,128)S(1)}, u32[]{:S(2)}, u32[]{:S(2)}) %collective-permute-start.7) | collective-permute-done | bytes 18464 | tf_op jit(solution)/shard_map/ppermute | solution.py:27
  180.9 1.8 collective-permute-done.6
  184.5 96.5 %all-reduce.1 = (f32[]{:T(128)}, f32[]{:T(128)}, f32[]{:T(128)}) all-reduce(f32[]{:T(128)} %get-tuple-element.11, f32[]{:T(128)} %get-tuple-element.10, f32[]{:T(128)} %get-tuple-element.9), channel_id=1, replica_groups=mesh['py'=8,'px'=32] {'py','px'}, use_global_device_ids=true, to_apply=%region_7.8 | all-reduce | flops 3 | bytes 24 | tf_op jit(solution)/shard_map/psum | solution.py:143
  283.6 0.9 multiply_reduce_fusion.6
  284.5 2.9 collective-permute-start.9
  287.4 2.7 collective-permute-start.8
  291.1 1.3 collective-permute-start.11
  292.4 4.2 collective-permute-start.10
  296.7 4.4 collective-permute-done.11
  301.1 0.9 collective-permute-done.10
  304.5 4.6 fusion.173
  309.7 5.4 %fusion.171 = f32[2,128,128,64]{2,3,1,0:T(8,128)} fusion(bf16[2,2,128,128]{3,1,2,0:T(2,128)(2,1)S(1)} %copy.26), kind=kOutput, calls=%fused_computation.251 | convolution fusion | flops 8390528 | bytes 8519680 | tf_op jit(solution)/shard_map/qz,bzgf->bqgf/dot_general | solution.py:41
  315.6 3.5 subtract_convert_fusion
  319.1 1.5 copy-done.6
  320.6 7.4 %fusion.3 = (bf16[2,64,128,128]{3,1,2,0:T(8,128)(2,1)S(1)}, bf16[2,64,128,128]{3,1,2,0:T(8,128)(2,1)S(1)}) fusion(bf16[2,128,128,64]{2,3,1,0:T(8,128)(2,1)} %subtract_convert_fusion, f32[64,128,128]{2,0,1:T(8,128)S(1)} %copy-done.6, f32[64,128,128]{2,0,1:T(8,128)S(1)} %copy-done.3, f32[2,128,128,64]{2,3,1,0:T(8,128)} %fusion.171, ...), kind=kOutput, calls=%fused_computation.5 | convolution fusion | flops 33556480 | bytes 29491200 | tf_op jit(solution)/shard_map/qz,bzgf->bqgf/dot_general | solution.py:41
  331.1 2.9 fusion.31
  335.7 2.8 collective-permute-start.13
  338.5 2.8 collective-permute-start.12
  342.3 1.3 collective-permute-start.15
  343.6 5.0 %collective-permute-start.14 = (f32[2,2,144,8]{3,2,1,0:T(8,128)S(1)}, f32[2,2,144,8]{3,2,1,0:T(8,128)S(1)}, u32[]{:S(2)}, u32[]{:S(2)}) collective-permute-start(f32[2,2,144,8]{3,2,1,0:T(8,128)S(1)} %get-tuple-element.41), channel_id=1, source_target_pairs={{0,1},{1,2},{2,3},{3,4},{4,5},{5,6},{6,7},{7,8},{8,9},{9,10},{10,1... | collective-permute-start | bytes 55304 | tf_op jit(solution)/shard_map/ppermute | solution.py:26
  349.5 4.1 collective-permute-done.15
  353.6 1.5 collective-permute-done.14
  357.0 102.0 %all-reduce = (f32[]{:T(128)}, f32[]{:T(128)}, f32[]{:T(128)}) all-reduce(f32[]{:T(128)} %get-tuple-element.7, f32[]{:T(128)} %get-tuple-element.8, f32[]{:T(128)} %get-tuple-element.6), channel_id=1, replica_groups=mesh['py'=8,'px'=32] {'py','px'}, use_global_device_ids=true, to_apply=%region_13.14 | all-reduce | flops 3 | bytes 24 | tf_op jit(solution)/shard_map/psum | solution.py:157
  (145 shorter events, 30.5 us)
Async XLA Ops:
  0.6 95.4 %copy-start = (bf16[1,1,32,32,32]{4,3,2,1,0:T(8,128)(2,1)S(1)}, bf16[1,1,32,32,32]{4,3,2,1,0:T(8,128)(2,1)}, u32[]{:S(2)}) copy-start(bf16[1,1,32,32,32]{4,3,2,1,0:T(8,128)(2,1)} %param.5) | copy-start | bytes 196612
  88.6 10.1 %copy-start.12 = (bf16[2,2,112,112]{3,2,1,0:T(8,128)(2,1)}, bf16[2,2,112,112]{3,2,1,0:T(8,128)(2,1)S(1)}, u32[]{:S(2)}) copy-start(bf16[2,2,112,112]{3,2,1,0:T(8,128)(2,1)S(1)} %constant_dynamic-update-slice_fusion) | copy-start | bytes 301060
  88.6 25.8 %collective-permute-start.1 = (bf16[2,2,8,112]{3,2,1,0:T(8,128)(2,1)S(1)}, bf16[2,2,8,112]{3,2,1,0:T(8,128)(2,1)S(1)}, u32[]{:S(2)}, u32[]{:S(2)}) collective-permute-start(bf16[2,2,8,112]{3,2,1,0:T(8,128)(2,1)S(1)} %get-tuple-element.56), channel_id=1, source_target_pairs={{32,0},{64,32},{96,64},{128,96},{160,128},{192,160},{224,192},{33,... | collective-permute-start | bytes 21512 | tf_op jit(solution)/shard_map/ppermute | solution.py:27
  91.4 23.0 %collective-permute-start = (bf16[2,2,8,112]{3,2,1,0:T(8,128)(2,1)S(1)}, bf16[2,2,8,112]{3,2,1,0:T(8,128)(2,1)S(1)}, u32[]{:S(2)}, u32[]{:S(2)}) collective-permute-start(bf16[2,2,8,112]{3,2,1,0:T(8,128)(2,1)S(1)} %get-tuple-element.55), channel_id=1, source_target_pairs={{0,32},{32,64},{64,96},{96,128},{128,160},{160,192},{192,224},{1,3... | collective-permute-start | bytes 21512 | tf_op jit(solution)/shard_map/ppermute | solution.py:26
  96.4 1.1 copy-start.10
  98.1 4.1 copy-start.11
  111.5 2.9 copy-start.13
  111.5 19.0 %copy-start.15 = (s32[128,128]{1,0:T(8,128)S(1)}, s32[128,128]{1,0:T(8,128)}, u32[]{:S(2)}) copy-start(s32[128,128]{1,0:T(8,128)} %param.7) | copy-start | bytes 196612
  114.6 16.0 %collective-permute-start.3 = (bf16[2,2,128,8]{3,2,1,0:T(8,128)(2,1)S(1)}, bf16[2,2,128,8]{3,2,1,0:T(8,128)(2,1)S(1)}, u32[]{:S(2)}, u32[]{:S(2)}) collective-permute-start(bf16[2,2,128,8]{3,2,1,0:T(8,128)(2,1)S(1)} %get-tuple-element.54), channel_id=1, source_target_pairs={{1,0},{2,1},{3,2},{4,3},{5,4},{6,5},{7,6},{8,7},{9,8},{10,9},{11,1... | collective-permute-start | bytes 24584 | tf_op jit(solution)/shard_map/ppermute | solution.py:27
  115.9 14.7 %collective-permute-start.2 = (bf16[2,2,128,8]{3,2,1,0:T(8,128)(2,1)S(1)}, bf16[2,2,128,8]{3,2,1,0:T(8,128)(2,1)S(1)}, u32[]{:S(2)}, u32[]{:S(2)}) collective-permute-start(bf16[2,2,128,8]{3,2,1,0:T(8,128)(2,1)S(1)} %get-tuple-element.53), channel_id=1, source_target_pairs={{0,1},{1,2},{2,3},{3,4},{4,5},{5,6},{6,7},{7,8},{8,9},{9,10},{10,1... | collective-permute-start | bytes 24584 | tf_op jit(solution)/shard_map/ppermute | solution.py:26
  138.2 5.9 %copy-start.8 = (f32[2,128,128,64]{2,3,1,0:T(8,128)S(1)}, f32[2,128,128,64]{2,3,1,0:T(8,128)}, u32[]{:S(2)}) copy-start(f32[2,128,128,64]{2,3,1,0:T(8,128)} %fusion.177) | copy-start | bytes 25165828
  144.1 3.5 copy-start.2
  144.1 5.0 %copy-start.7 = (f32[64,128,128]{2,0,1:T(8,128)S(1)}, f32[64,128,128]{2,0,1:T(8,128)}, u32[]{:S(2)}) copy-start(f32[64,128,128]{2,0,1:T(8,128)} %get-tuple-element.59) | copy-start | bytes 12582916
  156.5 1.9 copy-start.5
  164.2 5.6 %collective-permute-start.5 = (f32[2,2,8,128]{3,2,1,0:T(8,128)S(1)}, f32[2,2,8,128]{3,2,1,0:T(8,128)S(1)}, u32[]{:S(2)}, u32[]{:S(2)}) collective-permute-start(f32[2,2,8,128]{3,2,1,0:T(8,128)S(1)} %get-tuple-element.50), channel_id=1, source_target_pairs={{32,0},{64,32},{96,64},{128,96},{160,128},{192,160},{224,192},{33,... | collective-permute-start | bytes 49160 | tf_op jit(solution)/shard_map/ppermute | solution.py:27
  166.4 4.3 collective-permute-start.4
  170.8 10.1 %collective-permute-start.7 = (f32[2,2,144,8]{3,2,1,0:T(8,128)S(1)}, f32[2,2,144,8]{3,2,1,0:T(8,128)S(1)}, u32[]{:S(2)}, u32[]{:S(2)}) collective-permute-start(f32[2,2,144,8]{3,2,1,0:T(8,128)S(1)} %get-tuple-element.44), channel_id=1, source_target_pairs={{1,0},{2,1},{3,2},{4,3},{5,4},{6,5},{7,6},{8,7},{9,8},{10,9},{11,1... | collective-permute-start | bytes 55304 | tf_op jit(solution)/shard_map/ppermute | solution.py:27
  172.1 10.5 %collective-permute-start.6 = (f32[2,2,144,8]{3,2,1,0:T(8,128)S(1)}, f32[2,2,144,8]{3,2,1,0:T(8,128)S(1)}, u32[]{:S(2)}, u32[]{:S(2)}) collective-permute-start(f32[2,2,144,8]{3,2,1,0:T(8,128)S(1)} %get-tuple-element.43), channel_id=1, source_target_pairs={{0,1},{1,2},{2,3},{3,4},{4,5},{5,6},{6,7},{7,8},{8,9},{9,10},{10,1... | collective-permute-start | bytes 55304 | tf_op jit(solution)/shard_map/ppermute | solution.py:26
  183.0 100.6 %copy-start.14 = (f32[1,2,1,1,12544]{4,3,2,1,0:T(1,128)S(1)}, f32[1,2,1,1,12544]{4,3,2,1,0:T(1,128)}, u32[]{:S(2)}) copy-start(f32[1,2,1,1,12544]{4,3,2,1,0:T(1,128)} %get-tuple-element.31) | copy-start | bytes 301060
  284.5 6.5 %collective-permute-start.9 = (f32[2,2,8,112]{3,2,1,0:T(8,128)S(1)}, f32[2,2,8,112]{3,2,1,0:T(8,128)S(1)}, u32[]{:S(2)}, u32[]{:S(2)}) collective-permute-start(f32[2,2,8,112]{3,2,1,0:T(8,128)S(1)} %get-tuple-element.52), channel_id=1, source_target_pairs={{32,0},{64,32},{96,64},{128,96},{160,128},{192,160},{224,192},{33,... | collective-permute-start | bytes 43016 | tf_op jit(solution)/shard_map/ppermute | solution.py:27
  287.4 3.6 collective-permute-start.8
  291.1 10.0 %collective-permute-start.11 = (f32[2,2,128,8]{3,2,1,0:T(8,128)S(1)}, f32[2,2,128,8]{3,2,1,0:T(8,128)S(1)}, u32[]{:S(2)}, u32[]{:S(2)}) collective-permute-start(f32[2,2,128,8]{3,2,1,0:T(8,128)S(1)} %get-tuple-element.48), channel_id=1, source_target_pairs={{1,0},{2,1},{3,2},{4,3},{5,4},{6,5},{7,6},{8,7},{9,8},{10,9},{11,1... | collective-permute-start | bytes 49160 | tf_op jit(solution)/shard_map/ppermute | solution.py:27
  292.4 9.6 %collective-permute-start.10 = (f32[2,2,128,8]{3,2,1,0:T(8,128)S(1)}, f32[2,2,128,8]{3,2,1,0:T(8,128)S(1)}, u32[]{:S(2)}, u32[]{:S(2)}) collective-permute-start(f32[2,2,128,8]{3,2,1,0:T(8,128)S(1)} %get-tuple-element.47), channel_id=1, source_target_pairs={{0,1},{1,2},{2,3},{3,4},{4,5},{5,6},{6,7},{7,8},{8,9},{9,10},{10,1... | collective-permute-start | bytes 49160 | tf_op jit(solution)/shard_map/ppermute | solution.py:26
  309.7 5.9 %copy-start.9 = (f32[2,128,128,64]{2,3,1,0:T(8,128)S(1)}, f32[2,128,128,64]{2,3,1,0:T(8,128)}, u32[]{:S(2)}) copy-start(f32[2,128,128,64]{2,3,1,0:T(8,128)} %fusion.173) | copy-start | bytes 25165828
  315.6 3.5 copy-start.3
  315.6 5.0 %copy-start.6 = (f32[64,128,128]{2,0,1:T(8,128)S(1)}, f32[64,128,128]{2,0,1:T(8,128)}, u32[]{:S(2)}) copy-start(f32[64,128,128]{2,0,1:T(8,128)} %get-tuple-element.60) | copy-start | bytes 12582916
  328.0 1.9 copy-start.4
  335.7 5.6 %collective-permute-start.13 = (f32[2,2,8,128]{3,2,1,0:T(8,128)S(1)}, f32[2,2,8,128]{3,2,1,0:T(8,128)S(1)}, u32[]{:S(2)}, u32[]{:S(2)}) collective-permute-start(f32[2,2,8,128]{3,2,1,0:T(8,128)S(1)} %get-tuple-element.46), channel_id=1, source_target_pairs={{32,0},{64,32},{96,64},{128,96},{160,128},{192,160},{224,192},{33,... | collective-permute-start | bytes 49160 | tf_op jit(solution)/shard_map/ppermute | solution.py:27
  338.5 3.6 collective-permute-start.12
  342.3 11.3 %collective-permute-start.15 = (f32[2,2,144,8]{3,2,1,0:T(8,128)S(1)}, f32[2,2,144,8]{3,2,1,0:T(8,128)S(1)}, u32[]{:S(2)}, u32[]{:S(2)}) collective-permute-start(f32[2,2,144,8]{3,2,1,0:T(8,128)S(1)} %get-tuple-element.42), channel_id=1, source_target_pairs={{1,0},{2,1},{3,2},{4,3},{5,4},{6,5},{7,6},{8,7},{9,8},{10,9},{11,1... | collective-permute-start | bytes 55304 | tf_op jit(solution)/shard_map/ppermute | solution.py:27
  343.6 11.5 %collective-permute-start.14 = (f32[2,2,144,8]{3,2,1,0:T(8,128)S(1)}, f32[2,2,144,8]{3,2,1,0:T(8,128)S(1)}, u32[]{:S(2)}, u32[]{:S(2)}) collective-permute-start(f32[2,2,144,8]{3,2,1,0:T(8,128)S(1)} %get-tuple-element.41), channel_id=1, source_target_pairs={{0,1},{1,2},{2,3},{3,4},{4,5},{5,6},{6,7},{7,8},{8,9},{9,10},{10,1... | collective-permute-start | bytes 55304 | tf_op jit(solution)/shard_map/ppermute | solution.py:26
  355.1 108.0 %copy-start.1 = (bf16[1,1,32,32,32]{4,3,2,1,0:T(8,128)(2,1)S(1)}, bf16[1,1,32,32,32]{4,3,2,1,0:T(8,128)(2,1)}, u32[]{:S(2)}) copy-start(bf16[1,1,32,32,32]{4,3,2,1,0:T(8,128)(2,1)} %param.5) | copy-start | bytes 196612
where the time goes:
time: 469 us; the launch traced here: 464 us
  blocking collectives  280 us (60%)
  matrix products  74.1 us (16%)
  starting transfers between devices  55.3 us (12%)
  waiting for transfers between devices  19 us (4%)
  local copies, waits for them, and re-layouts  14.9 us (3%)
  other arithmetic  10.9 us (2%)
  between operations  9.35 us (2%)
    psum x1, blocking collectives, body(): beta_terms = lax.psum((third_sq, third_cross, third_tail), ('py', 'px'))  102 us
    psum x1, blocking collectives, body(): alpha_terms = lax.psum((second_sq, second_cross, second_tail), ('py', 'px'))  96.5 us
    psum x1, blocking collectives, body(): start_terms = lax.psum((first_sq, first_cross, first_tail), ('py', 'px'))  81.5 us
    dot_general x46, matrix products, product(): return jnp.einsum(form, table, values, preferred_element_type=jnp.float32)  74.1 us
    ppermute x8, starting transfers between devices, padded_2(): before = lax.ppermute(last, axis, up)  39.4 us
    ppermute x8, starting transfers between devices, padded_2(): after = lax.ppermute(leading, axis, down)  15.9 us
    ppermute x8, waiting for transfers between devices, padded_2(): after = lax.ppermute(leading, axis, down)  13.2 us
  transfers between devices with their start and end apart: 16, of which 8 were waited for; matrix products, arithmetic and copies ran while one was open for 4% of the time, Pallas kernels for 0%

commit v1 on v0

--- a/solution.py
+++ b/solution.py
@@ -1,8 +1,12 @@
+import functools
 import math
 
 import jax
 import jax.numpy as jnp
+import numpy as np
 from jax import lax
+from jax.experimental import pallas as pl
+from jax.experimental.pallas import tpu as pltpu
 from jax.sharding import PartitionSpec as P
 
 PLANES = 2
@@ -29,12 +33,23 @@
     return shard
 
 
-def twiddle(rows, cols, length, shift):
-    row_ids = jnp.arange(rows, dtype=jnp.int32)[:, None]
-    col_ids = jnp.arange(cols, dtype=jnp.int32)[None, :] + jnp.asarray(shift).astype(jnp.int32)
-    phase = row_ids * col_ids % length
-    angle = phase.astype(jnp.float32) * jnp.float32(2.0 * math.pi / length)
-    return (jnp.cos(angle).astype(jnp.bfloat16), (-jnp.sin(angle)).astype(jnp.bfloat16))
+def roots(rows, cols, length):
+    phase = np.outer(np.asarray(rows), np.asarray(cols)) % length
+    angle = phase * (2.0 * math.pi / length)
+    return (np.cos(angle).astype(jnp.bfloat16), (-np.sin(angle)).astype(jnp.bfloat16))
+
+
+def depth_mix():
+    shifted = np.arange(KERNEL) - KERNEL // 2
+    depths = np.arange(DEPTH_LEN)
+    cos_t, sin_t = (part.astype(np.float64) for part in roots(depths, shifted, DEPTH_LEN))
+    cos_z, sin_z = (
+        part.astype(np.float64) for part in roots(depths, np.arange(PLANES), DEPTH_LEN)
+    )
+    taps = cos_t + 1j * sin_t
+    ahead = cos_z + 1j * sin_z
+    mix = np.einsum("qo,qz,qt->ozt", np.conj(ahead), ahead, taps)
+    return np.stack([mix.real, mix.imag]).astype(np.float32)
 
 
 def product(form, table, values):
@@ -44,41 +59,160 @@
 def complex_axis(form, cos_table, sin_table, real_in, imag_in):
     real_out = product(form, cos_table, real_in) - product(form, sin_table, imag_in)
     imag_out = product(form, cos_table, imag_in) + product(form, sin_table, real_in)
-    return (real_out.astype(jnp.bfloat16), imag_out.astype(jnp.bfloat16))
+    return (real_out, imag_out)
+
+
+def narrow(pair):
+    return (pair[0].astype(jnp.bfloat16), pair[1].astype(jnp.bfloat16))
+
+
+def shifted_roots(shift):
+    half_kernel = KERNEL // 2
+    cos_all, sin_all = roots(np.arange(KERNEL + 8) - half_kernel, np.arange(PATCH), PATCH)
+    return (
+        lax.dynamic_slice_in_dim(jnp.asarray(cos_all), shift, KERNEL, axis=0),
+        lax.dynamic_slice_in_dim(jnp.asarray(sin_all), shift, KERNEL, axis=0),
+    )
 
 
 def spectrum(patch_taps, shift_rows, shift_cols):
-    half_kernel = KERNEL // 2
-    cos_x, sin_x = twiddle(PATCH, KERNEL, PATCH, shift_cols - half_kernel)
-    real_x = product("fi,tji->tjf", cos_x, patch_taps).astype(jnp.bfloat16)
-    imag_x = product("fi,tji->tjf", sin_x, patch_taps).astype(jnp.bfloat16)
-    cos_y, sin_y = twiddle(PATCH, KERNEL, PATCH, shift_rows - half_kernel)
-    real_y, imag_y = complex_axis("gj,tjf->tgf", cos_y, sin_y, real_x, imag_x)
-    cos_z, sin_z = twiddle(DEPTH_LEN, KERNEL, DEPTH_LEN, -half_kernel)
-    return complex_axis("qt,tgf->qgf", cos_z, sin_z, real_y, imag_y)
+    mixed = jnp.einsum(
+        "cozt,tji->cozji",
+        depth_mix(),
+        patch_taps.astype(jnp.float32),
+        precision=lax.Precision.HIGHEST,
+    )
+    mixed_re, mixed_im = narrow((mixed[0], mixed[1]))
+    cos_x, sin_x = shifted_roots(shift_cols)
+    real_x, imag_x = narrow(complex_axis("if,ozji->ozjf", cos_x, sin_x, mixed_re, mixed_im))
+    cos_y, sin_y = shifted_roots(shift_rows)
+    return complex_axis("jg,ozjf->ozgf", cos_y, sin_y, real_x, imag_x)
 
 
 def blur(patch_cells, spec_real, spec_imag, adjoint):
     values = patch_cells.astype(jnp.bfloat16)
-    cos_p, sin_p = twiddle(PATCH, PATCH, PATCH, 0)
+    cos_p, sin_p = roots(np.arange(PATCH), np.arange(PATCH), PATCH)
     real_x = product("fx,bzyx->bzyf", cos_p, values).astype(jnp.bfloat16)
     imag_x = product("fx,bzyx->bzyf", sin_p, values).astype(jnp.bfloat16)
     real_y, imag_y = complex_axis("gy,bzyf->bzgf", cos_p, sin_p, real_x, imag_x)
-    cos_z, sin_z = twiddle(DEPTH_LEN, PLANES, DEPTH_LEN, 0)
-    depth_re, depth_im = complex_axis("qz,bzgf->bqgf", cos_z, sin_z, real_y, imag_y)
-    kernel_re = spec_real.astype(jnp.float32)
-    kernel_im = spec_imag.astype(jnp.float32)
-    if adjoint:
-        kernel_im = -kernel_im
-    depth_re = depth_re.astype(jnp.float32)
-    depth_im = depth_im.astype(jnp.float32)
-    prod_re = (depth_re * kernel_re - depth_im * kernel_im).astype(jnp.bfloat16)
-    prod_im = (depth_re * kernel_im + depth_im * kernel_re).astype(jnp.bfloat16)
-    back_cos, back_sin = twiddle(PLANES, DEPTH_LEN, DEPTH_LEN, 0)
-    plane_re, plane_im = complex_axis("zq,bqgf->bzgf", back_cos, -back_sin, prod_re, prod_im)
-    row_re, row_im = complex_axis("yg,bzgf->bzyf", cos_p, -sin_p, plane_re, plane_im)
+    planes_re, planes_im = [], []
+    for out in range(PLANES):
+        total_re, total_im = 0.0, 0.0
+        for z in range(PLANES):
+            if adjoint:
+                kernel_re, kernel_im = spec_real[z, out], -spec_imag[z, out]
+            else:
+                kernel_re, kernel_im = spec_real[out, z], spec_imag[out, z]
+            total_re = total_re + real_y[:, z] * kernel_re - imag_y[:, z] * kernel_im
+            total_im = total_im + real_y[:, z] * kernel_im + imag_y[:, z] * kernel_re
+        planes_re.append(total_re)
+        planes_im.append(total_im)
+    plane_re, plane_im = narrow((jnp.stack(planes_re, axis=1), jnp.stack(planes_im, axis=1)))
+    row_re, row_im = narrow(complex_axis("yg,bzgf->bzyf", cos_p, -sin_p, plane_re, plane_im))
     spatial = product("xf,bzyf->bzyx", cos_p, row_re) + product("xf,bzyf->bzyx", sin_p, row_im)
     return spatial * jnp.float32(1.0 / (DEPTH_LEN * PATCH * PATCH))
+
+
+def gather_kernel(rows, cols, x_ref, out_ref, first, mid, second, send_r, recv_r, send_c, recv_c):
+    my_row, my_col = lax.axis_index("py"), lax.axis_index("px")
+    barrier = pltpu.get_barrier_semaphore()
+
+    def greet_row(step, carry):
+        pl.semaphore_signal(
+            barrier,
+            inc=1,
+            device_id=((my_row + step) % rows, my_col),
+            device_id_type=pl.DeviceIdType.MESH,
+        )
+        return carry
+
+    def greet_col(step, carry):
+        pl.semaphore_signal(
+            barrier,
+            inc=1,
+            device_id=(my_row, (my_col + step) % cols),
+            device_id_type=pl.DeviceIdType.MESH,
+        )
+        return carry
+
+    lax.fori_loop(1, rows, greet_row, 0)
+    lax.fori_loop(1, cols, greet_col, 0)
+    pl.semaphore_wait(barrier, rows + cols - 2)
+
+    def row_copy(step):
+        return pltpu.make_async_remote_copy(
+            src_ref=x_ref,
+            dst_ref=first.at[step],
+            send_sem=send_r.at[step],
+            recv_sem=recv_r.at[step],
+            device_id=((my_row + step) % rows, my_col),
+            device_id_type=pl.DeviceIdType.MESH,
+        )
+
+    def col_copy(step):
+        return pltpu.make_async_remote_copy(
+            src_ref=mid,
+            dst_ref=second.at[step],
+            send_sem=send_c.at[step],
+            recv_sem=recv_c.at[step],
+            device_id=(my_row, (my_col + step) % cols),
+            device_id_type=pl.DeviceIdType.MESH,
+        )
+
+    def start(copy):
+        def run(step, carry):
+            copy(step).start()
+            return carry
+
+        return run
+
+    def finish(copy):
+        def run(step, carry):
+            copy(step).wait()
+            return carry
+
+        return run
+
+    def ordered(own, slots, mine, size):
+        def run(index, total):
+            slot = (mine - index + size) % size
+            return total + slots[slot]
+
+        return lax.fori_loop(0, size, run, jnp.zeros_like(own))
+
+    lax.fori_loop(1, rows, start(row_copy), 0)
+    first[0] = x_ref[...]
+    lax.fori_loop(1, rows, finish(row_copy), 0)
+    summed = ordered(x_ref[...], first, my_row, rows)
+    mid[...] = summed
+    second[0] = summed
+    lax.fori_loop(1, cols, start(col_copy), 0)
+    lax.fori_loop(1, cols, finish(col_copy), 0)
+    out_ref[...] = ordered(summed, second, my_col, cols)
+
+
+def total_sum(terms):
+    rows, cols = lax.axis_size("py"), lax.axis_size("px")
+    lane = lax.broadcasted_iota(jnp.int32, (8, PATCH), 1)
+    tile = jnp.where(lane == 0, terms[0], jnp.where(lane == 1, terms[1], terms[2]))
+    tile = pl.pallas_call(
+        functools.partial(gather_kernel, rows, cols),
+        out_shape=jax.ShapeDtypeStruct((8, PATCH), jnp.float32),
+        in_specs=[pl.BlockSpec(memory_space=pltpu.VMEM)],
+        out_specs=pl.BlockSpec(memory_space=pltpu.VMEM),
+        scratch_shapes=[
+            pltpu.VMEM((rows, 8, PATCH), jnp.float32),
+            pltpu.VMEM((8, PATCH), jnp.float32),
+            pltpu.VMEM((cols, 8, PATCH), jnp.float32),
+            pltpu.SemaphoreType.DMA((rows,)),
+            pltpu.SemaphoreType.DMA((rows,)),
+            pltpu.SemaphoreType.DMA((cols,)),
+            pltpu.SemaphoreType.DMA((cols,)),
+        ],
+        compiler_params=pltpu.CompilerParams(collective_id=0, has_side_effects=True),
+        name="gather_sum",
+    )(tile)
+    return (tile[0, 0], tile[0, 1], tile[0, 2])
 
 
 def window(mask_block):
@@ -130,7 +264,7 @@
     spec_real, spec_imag = spectrum(psf_taps[0, 0], offsets[0, 0, 0], offsets[0, 0, 1])
     weight = window(window_mask)
     first_sq, first_cross, first_tail = gram_terms(measured)
-    start_terms = lax.psum((first_sq, first_cross, first_tail), ("py", "px"))
+    start_terms = total_sum((first_sq, first_cross, first_tail))
     start_factor = factor(start_terms, count)
     left_flat = solve_right(measured, start_factor)
     left_basis = left_flat.reshape(2, PLANES, CORE, CORE)
@@ -140,7 +274,7 @@
     folded = padded_2(adjoint_patch, (("py", 2), ("px", 3)), HALF)
     adjoint_core = fold_owned(fold_owned(folded, 2), 3)
     second_sq, second_cross, second_tail = gram_terms(adjoint_core)
-    alpha_terms = lax.psum((second_sq, second_cross, second_tail), ("py", "px"))
+    alpha_terms = total_sum((second_sq, second_cross, second_tail))
     alpha_factor = factor(alpha_terms, count)
     object_basis = solve_right(adjoint_core, alpha_factor)
     object_patch = padded_2(object_basis, (("py", 2), ("px", 3)), HALF)
@@ -154,7 +288,7 @@
         ]
     )
     third_sq, third_cross, third_tail = gram_terms(residue)
-    beta_terms = lax.psum((third_sq, third_cross, third_tail), ("py", "px"))
+    beta_terms = total_sum((third_sq, third_cross, third_tail))
     beta_factor = factor(beta_terms, count)
     image_basis = solve_right(residue, beta_factor)
     factors = jnp.stack([packed(start_factor), packed(alpha_factor), packed(beta_factor)])

time: 469 us -> 233 us (0.50)
  blocking collectives: 280 us -> 0 us
  Pallas kernels: 0 us -> 106 us
  matrix products: 74.1 us -> 6.27 us
  waiting for transfers between devices: 19 us -> 36.1 us
  starting transfers between devices: 55.3 us -> 41.1 us
  other arithmetic: 10.9 us -> 17.3 us
    psum x3 -> x0, blocking collectives: 280 us -> none  [the longest x1 102 us: body(): beta_terms = lax.psum((third_sq, third_cross, third_tail), ('py', 'px'))]
    pallas_call x0 -> x3, Pallas kernels: none -> 106 us  [total_sum(): pl.pallas_call(functools.partial(gather_kernel, rows, cols), out_shape=ja...]
    dot_general x46 -> x28, matrix products: 74.1 us -> 5.96 us  [product(): return jnp.einsum(form, table, values, preferred_element_type=jnp.float32)]
    ppermute x8, waiting for transfers between devices: 13.2 us -> 25.4 us  [padded_2(): after = lax.ppermute(leading, axis, down)]
    ppermute x8, starting transfers between devices: 39.4 us -> 28.1 us  [padded_2(): before = lax.ppermute(last, axis, up)]
    select_n x0 -> x6, other arithmetic: none -> 7.52 us  [the longest x3 3.79 us: total_sum(): jnp.where(lane == 1, terms[1], terms[2])]
    convert_element_type x10 -> x1, local copies, waits for them, and re-layouts: 4.89 us -> 0.05 us  [narrow(): return (pair[0].astype(jnp.bfloat16), pair[1].astype(jnp.bfloat16))]
    ppermute x8, waiting for transfers between devices: 5.83 us -> 10.7 us  [padded_2(): before = lax.ppermute(last, axis, up)]
  transfers between devices with their start and end apart: 16 -> 16, of which waited for: 8 -> 11; matrix products, arithmetic and copies ran while one was open for 4% -> 2% of each run, Pallas kernels for 0% -> 0%
where the time goes in v1:
time: 233 us; the launch traced here: 231 us
  Pallas kernels  106 us (45%)
  starting transfers between devices  41.1 us (18%)
  waiting for transfers between devices  36.1 us (15%)
  other arithmetic  17.3 us (7%)
  local copies, waits for them, and re-layouts  13.4 us (6%)
  between operations  11.4 us (5%)
  matrix products  6.27 us (3%)
    pallas_call x3, Pallas kernels, total_sum(): pl.pallas_call(functools.partial(gather_kernel, rows, cols), out_shape=ja...  106 us
    ppermute x8, starting transfers between devices, padded_2(): before = lax.ppermute(last, axis, up)  28.1 us
    ppermute x8, waiting for transfers between devices, padded_2(): after = lax.ppermute(leading, axis, down)  25.4 us
    ppermute x8, starting transfers between devices, padded_2(): after = lax.ppermute(leading, axis, down)  13 us
    ppermute x8, waiting for transfers between devices, padded_2(): before = lax.ppermute(last, axis, up)  10.7 us
    dot_general x28, matrix products, product(): return jnp.einsum(form, table, values, preferred_element_type=jnp.float32)  5.96 us
  transfers between devices with their start and end apart: 16, of which 11 were waited for; matrix products, arithmetic and copies ran while one was open for 2% of the time, Pallas kernels for 0%

profile of v1, /device:TPU:1, one launch (start us, length us, event | category | flops | bytes accessed | tf_op | source)
XLA Modules:
  0.0 231.2 jit_solution(1181706069642324546)
XLA Ops:
  0.7 1.9 multiply_reduce_fusion.11
  2.5 1.3 fusion.64
  3.8 1.2 broadcast_select_fusion.2.x_ref
  5.1 23.4 %gather_sum.3 = f32[8,128]{1,0:T(8,128)} custom-call(f32[8,128]{1,0:T(8,128)} %broadcast_select_fusion.2.x_ref), custom_call_target="tpu_custom_call" | custom-call | tf_op jit(solution)/shard_map/gather_sum/pallas_call | solution.py:198
  28.5 1.4 fusion.90
  33.0 4.9 %collective-permute-start = (bf16[2,2,8,112]{3,2,1,0:T(8,128)(2,1)S(1)}, bf16[2,2,8,112]{3,2,1,0:T(8,128)(2,1)S(1)}, u32[]{:S(2)}, u32[]{:S(2)}) collective-permute-start(bf16[2,2,8,112]{3,2,1,0:T(8,128)(2,1)S(1)} %get-tuple-element.62), channel_id=1, source_target_pairs={{0,32},{32,64},{64,96},{96,128},{128,160},{160,192},{192,224},{1,3... | collective-permute-start | bytes 21512 | tf_op jit(solution)/shard_map/ppermute | solution.py:30
  38.0 1.9 collective-permute-start.1
  46.9 2.5 %collective-permute-start.2 = (bf16[2,2,128,8]{3,2,1,0:T(8,128)(2,1)S(1)}, bf16[2,2,128,8]{3,2,1,0:T(8,128)(2,1)S(1)}, u32[]{:S(2)}, u32[]{:S(2)}) collective-permute-start(bf16[2,2,128,8]{3,2,1,0:T(8,128)(2,1)S(1)} %get-tuple-element.60), channel_id=1, source_target_pairs={{0,1},{1,2},{2,3},{3,4},{4,5},{5,6},{6,7},{7,8},{8,9},{9,10},{10,1... | collective-permute-start | bytes 24584 | tf_op jit(solution)/shard_map/ppermute | solution.py:30
  49.4 1.3 collective-permute-start.3
  51.3 3.8 %collective-permute-done.3 = bf16[2,2,128,8]{3,2,1,0:T(8,128)(2,1)S(1)} collective-permute-done((bf16[2,2,128,8]{3,2,1,0:T(8,128)(2,1)S(1)}, bf16[2,2,128,8]{3,2,1,0:T(8,128)(2,1)S(1)}, u32[]{:S(2)}, u32[]{:S(2)}) %collective-permute-start.3) | collective-permute-done | bytes 8224 | tf_op jit(solution)/shard_map/ppermute | solution.py:31
  59.0 5.1 %collective-permute-start.4 = (f32[2,2,8,128]{3,2,1,0:T(8,128)S(1)}, f32[2,2,8,128]{3,2,1,0:T(8,128)S(1)}, u32[]{:S(2)}, u32[]{:S(2)}) collective-permute-start(f32[2,2,8,128]{3,2,1,0:T(8,128)S(1)} %get-tuple-element.48), channel_id=1, source_target_pairs={{0,32},{32,64},{64,96},{96,128},{128,160},{160,192},{192,224},{1,3... | collective-permute-start | bytes 49160 | tf_op jit(solution)/shard_map/ppermute | solution.py:30
  64.0 1.9 collective-permute-start.5
  66.0 3.1 %collective-permute-done.5 = f32[2,2,8,128]{3,2,1,0:T(8,128)S(1)} collective-permute-done((f32[2,2,8,128]{3,2,1,0:T(8,128)S(1)}, f32[2,2,8,128]{3,2,1,0:T(8,128)S(1)}, u32[]{:S(2)}, u32[]{:S(2)}) %collective-permute-start.5) | collective-permute-done | bytes 16416 | tf_op jit(solution)/shard_map/ppermute | solution.py:31
  69.3 3.1 %collective-permute-start.6 = (f32[2,2,144,8]{3,2,1,0:T(8,128)S(1)}, f32[2,2,144,8]{3,2,1,0:T(8,128)S(1)}, u32[]{:S(2)}, u32[]{:S(2)}) collective-permute-start(f32[2,2,144,8]{3,2,1,0:T(8,128)S(1)} %get-tuple-element.38), channel_id=1, source_target_pairs={{0,1},{1,2},{2,3},{3,4},{4,5},{5,6},{6,7},{7,8},{8,9},{9,10},{10,1... | collective-permute-start | bytes 55304 | tf_op jit(solution)/shard_map/ppermute | solution.py:30
  72.4 1.3 collective-permute-start.7
  73.7 3.9 %collective-permute-done.6 = f32[2,2,144,8]{3,2,1,0:T(8,128)S(1)} collective-permute-done((f32[2,2,144,8]{3,2,1,0:T(8,128)S(1)}, f32[2,2,144,8]{3,2,1,0:T(8,128)S(1)}, u32[]{:S(2)}, u32[]{:S(2)}) %collective-permute-start.6) | collective-permute-done | bytes 18464 | tf_op jit(solution)/shard_map/ppermute | solution.py:30
  77.6 4.9 %collective-permute-done.7 = f32[2,2,144,8]{3,2,1,0:T(8,128)S(1)} collective-permute-done((f32[2,2,144,8]{3,2,1,0:T(8,128)S(1)}, f32[2,2,144,8]{3,2,1,0:T(8,128)S(1)}, u32[]{:S(2)}, u32[]{:S(2)}) %collective-permute-start.7) | collective-permute-done | bytes 18464 | tf_op jit(solution)/shard_map/ppermute | solution.py:31
  82.8 0.8 copy-done.3
  83.9 0.9 slice-done
  86.0 1.3 fusion.63
  87.3 1.2 broadcast_select_fusion.1.x_ref
  88.6 39.8 %gather_sum.4 = f32[8,128]{1,0:T(8,128)} custom-call(f32[8,128]{1,0:T(8,128)} %broadcast_select_fusion.1.x_ref), custom_call_target="tpu_custom_call" | custom-call | tf_op jit(solution)/shard_map/gather_sum/pallas_call | solution.py:198
  128.4 1.4 fusion.89
  132.2 3.2 %collective-permute-start.8 = (f32[2,2,8,112]{3,2,1,0:T(8,128)S(1)}, f32[2,2,8,112]{3,2,1,0:T(8,128)S(1)}, u32[]{:S(2)}, u32[]{:S(2)}) collective-permute-start(f32[2,2,8,112]{3,2,1,0:T(8,128)S(1)} %get-tuple-element.58), channel_id=1, source_target_pairs={{0,32},{32,64},{64,96},{96,128},{128,160},{160,192},{192,224},{1,3... | collective-permute-start | bytes 43016 | tf_op jit(solution)/shard_map/ppermute | solution.py:30
  135.5 1.9 collective-permute-start.9
  137.4 0.9 multiply_reduce_fusion.6
  138.3 0.9 pad_maximum_fusion.9
  139.3 1.3 collective-permute-done.9
  140.7 3.6 %collective-permute-start.10 = (f32[2,2,128,8]{3,2,1,0:T(8,128)S(1)}, f32[2,2,128,8]{3,2,1,0:T(8,128)S(1)}, u32[]{:S(2)}, u32[]{:S(2)}) collective-permute-start(f32[2,2,128,8]{3,2,1,0:T(8,128)S(1)} %get-tuple-element.46), channel_id=1, source_target_pairs={{0,1},{1,2},{2,3},{3,4},{4,5},{5,6},{6,7},{7,8},{8,9},{9,10},{10,1... | collective-permute-start | bytes 49160 | tf_op jit(solution)/shard_map/ppermute | solution.py:30
  144.3 1.3 collective-permute-start.11
  145.6 3.3 %collective-permute-done.10 = f32[2,2,128,8]{3,2,1,0:T(8,128)S(1)} collective-permute-done((f32[2,2,128,8]{3,2,1,0:T(8,128)S(1)}, f32[2,2,128,8]{3,2,1,0:T(8,128)S(1)}, u32[]{:S(2)}, u32[]{:S(2)}) %collective-permute-start.10) | collective-permute-done | bytes 16416 | tf_op jit(solution)/shard_map/ppermute | solution.py:30
  148.9 4.1 %collective-permute-done.11 = f32[2,2,128,8]{3,2,1,0:T(8,128)S(1)} collective-permute-done((f32[2,2,128,8]{3,2,1,0:T(8,128)S(1)}, f32[2,2,128,8]{3,2,1,0:T(8,128)S(1)}, u32[]{:S(2)}, u32[]{:S(2)}) %collective-permute-start.11) | collective-permute-done | bytes 16416 | tf_op jit(solution)/shard_map/ppermute | solution.py:31
  155.8 2.5 %collective-permute-start.12 = (f32[2,2,8,128]{3,2,1,0:T(8,128)S(1)}, f32[2,2,8,128]{3,2,1,0:T(8,128)S(1)}, u32[]{:S(2)}, u32[]{:S(2)}) collective-permute-start(f32[2,2,8,128]{3,2,1,0:T(8,128)S(1)} %get-tuple-element.40), channel_id=1, source_target_pairs={{0,32},{32,64},{64,96},{96,128},{128,160},{160,192},{192,224},{1,3... | collective-permute-start | bytes 49160 | tf_op jit(solution)/shard_map/ppermute | solution.py:30
  158.3 1.9 collective-permute-start.13
  160.3 3.0 %collective-permute-done.13 = f32[2,2,8,128]{3,2,1,0:T(8,128)S(1)} collective-permute-done((f32[2,2,8,128]{3,2,1,0:T(8,128)S(1)}, f32[2,2,8,128]{3,2,1,0:T(8,128)S(1)}, u32[]{:S(2)}, u32[]{:S(2)}) %collective-permute-start.13) | collective-permute-done | bytes 16416 | tf_op jit(solution)/shard_map/ppermute | solution.py:31
  163.5 3.1 %collective-permute-start.14 = (f32[2,2,144,8]{3,2,1,0:T(8,128)S(1)}, f32[2,2,144,8]{3,2,1,0:T(8,128)S(1)}, u32[]{:S(2)}, u32[]{:S(2)}) collective-permute-start(f32[2,2,144,8]{3,2,1,0:T(8,128)S(1)} %get-tuple-element.36), channel_id=1, source_target_pairs={{0,1},{1,2},{2,3},{3,4},{4,5},{5,6},{6,7},{7,8},{8,9},{9,10},{10,1... | collective-permute-start | bytes 55304 | tf_op jit(solution)/shard_map/ppermute | solution.py:30
  166.7 1.5 collective-permute-start.15
  169.1 2.9 %collective-permute-done.14 = f32[2,2,144,8]{3,2,1,0:T(8,128)S(1)} collective-permute-done((f32[2,2,144,8]{3,2,1,0:T(8,128)S(1)}, f32[2,2,144,8]{3,2,1,0:T(8,128)S(1)}, u32[]{:S(2)}, u32[]{:S(2)}) %collective-permute-start.14) | collective-permute-done | bytes 18464 | tf_op jit(solution)/shard_map/ppermute | solution.py:30
  172.0 5.2 %collective-permute-done.15 = f32[2,2,144,8]{3,2,1,0:T(8,128)S(1)} collective-permute-done((f32[2,2,144,8]{3,2,1,0:T(8,128)S(1)}, f32[2,2,144,8]{3,2,1,0:T(8,128)S(1)}, u32[]{:S(2)}, u32[]{:S(2)}) %collective-permute-start.15) | collective-permute-done | bytes 18464 | tf_op jit(solution)/shard_map/ppermute | solution.py:31
  177.5 0.8 copy-done.4
  178.5 0.9 slice-done.1
  180.0 0.7 multiply_reduce_fusion.2
  180.7 1.2 fusion.62
  181.9 1.2 broadcast_select_fusion.x_ref
  183.1 42.5 %gather_sum.5 = f32[8,128]{1,0:T(8,128)} custom-call(f32[8,128]{1,0:T(8,128)} %broadcast_select_fusion.x_ref), custom_call_target="tpu_custom_call" | custom-call | tf_op jit(solution)/shard_map/gather_sum/pallas_call | solution.py:198
  225.6 1.4 fusion.88
  229.5 0.7 copy.53
  230.3 0.9 pad_maximum_fusion.10
  (127 shorter events, 16.6 us)
Async XLA Ops:
  0.6 42.3 %copy-start = (bf16[1,1,32,32,32]{4,3,2,1,0:T(8,128)(2,1)S(1)}, bf16[1,1,32,32,32]{4,3,2,1,0:T(8,128)(2,1)}, u32[]{:S(2)}) copy-start(bf16[1,1,32,32,32]{4,3,2,1,0:T(8,128)(2,1)} %param.34) | copy-start | bytes 196612
  0.6 31.3 %copy-start.5 = (f32[2,2,1,1,12544]{4,3,2,1,0:T(1,128)S(1)}, f32[2,2,1,1,12544]{4,3,2,1,0:T(1,128)}, u32[]{:S(2)}) copy-start(f32[2,2,1,1,12544]{4,3,2,1,0:T(1,128)} %param.33) | copy-start | bytes 602116
  33.0 6.9 %copy-start.11 = (s32[1,1,2]{2,1,0:T(1,128)S(1)}, s32[1,1,2]{2,1,0:T(1,128)}, u32[]{:S(2)}) copy-start(s32[1,1,2]{2,1,0:T(1,128)} %param.35) | copy-start | bytes 28
  33.0 13.7 %collective-permute-start = (bf16[2,2,8,112]{3,2,1,0:T(8,128)(2,1)S(1)}, bf16[2,2,8,112]{3,2,1,0:T(8,128)(2,1)S(1)}, u32[]{:S(2)}, u32[]{:S(2)}) collective-permute-start(bf16[2,2,8,112]{3,2,1,0:T(8,128)(2,1)S(1)} %get-tuple-element.62), channel_id=1, source_target_pairs={{0,32},{32,64},{64,96},{96,128},{128,160},{160,192},{192,224},{1,3... | collective-permute-start | bytes 21512 | tf_op jit(solution)/shard_map/ppermute | solution.py:30
  38.0 8.7 %collective-permute-start.1 = (bf16[2,2,8,112]{3,2,1,0:T(8,128)(2,1)S(1)}, bf16[2,2,8,112]{3,2,1,0:T(8,128)(2,1)S(1)}, u32[]{:S(2)}, u32[]{:S(2)}) collective-permute-start(bf16[2,2,8,112]{3,2,1,0:T(8,128)(2,1)S(1)} %get-tuple-element.63), channel_id=1, source_target_pairs={{32,0},{64,32},{96,64},{128,96},{160,128},{192,160},{224,192},{33,... | collective-permute-start | bytes 21512 | tf_op jit(solution)/shard_map/ppermute | solution.py:31
  41.6 1.3 copy-start.10
  43.3 0.7 copy-start.9
  44.1 0.7 copy-start.8
  46.7 4.0 %copy-start.7 = (s32[128,128]{1,0:T(8,128)S(1)}, s32[128,128]{1,0:T(8,128)}, u32[]{:S(2)}) copy-start(s32[128,128]{1,0:T(8,128)} %param.36) | copy-start | bytes 196612
  46.9 4.5 %collective-permute-start.2 = (bf16[2,2,128,8]{3,2,1,0:T(8,128)(2,1)S(1)}, bf16[2,2,128,8]{3,2,1,0:T(8,128)(2,1)S(1)}, u32[]{:S(2)}, u32[]{:S(2)}) collective-permute-start(bf16[2,2,128,8]{3,2,1,0:T(8,128)(2,1)S(1)} %get-tuple-element.60), channel_id=1, source_target_pairs={{0,1},{1,2},{2,3},{3,4},{4,5},{5,6},{6,7},{7,8},{8,9},{9,10},{10,1... | collective-permute-start | bytes 24584 | tf_op jit(solution)/shard_map/ppermute | solution.py:30
  49.4 5.7 %collective-permute-start.3 = (bf16[2,2,128,8]{3,2,1,0:T(8,128)(2,1)S(1)}, bf16[2,2,128,8]{3,2,1,0:T(8,128)(2,1)S(1)}, u32[]{:S(2)}, u32[]{:S(2)}) collective-permute-start(bf16[2,2,128,8]{3,2,1,0:T(8,128)(2,1)S(1)} %get-tuple-element.61), channel_id=1, source_target_pairs={{1,0},{2,1},{3,2},{4,3},{5,4},{6,5},{7,6},{8,7},{9,8},{10,9},{11,1... | collective-permute-start | bytes 24584 | tf_op jit(solution)/shard_map/ppermute | solution.py:31
  50.7 4.5 %copy-start.2 = (bf16[128,128,1,1]{1,0,3,2:T(8,128)(2,1)S(1)}, bf16[128,128,1,1]{1,0,3,2:T(8,128)(2,1)}, u32[]{:S(2)}) copy-start(bf16[128,128,1,1]{1,0,3,2:T(8,128)(2,1)} %constant.61) | copy-start | bytes 98308
  55.3 0.8 copy-start.1
  57.5 0.8 copy-start.6
  59.0 7.0 %collective-permute-start.4 = (f32[2,2,8,128]{3,2,1,0:T(8,128)S(1)}, f32[2,2,8,128]{3,2,1,0:T(8,128)S(1)}, u32[]{:S(2)}, u32[]{:S(2)}) collective-permute-start(f32[2,2,8,128]{3,2,1,0:T(8,128)S(1)} %get-tuple-element.48), channel_id=1, source_target_pairs={{0,32},{32,64},{64,96},{96,128},{128,160},{160,192},{192,224},{1,3... | collective-permute-start | bytes 49160 | tf_op jit(solution)/shard_map/ppermute | solution.py:30
  64.0 5.1 %collective-permute-start.5 = (f32[2,2,8,128]{3,2,1,0:T(8,128)S(1)}, f32[2,2,8,128]{3,2,1,0:T(8,128)S(1)}, u32[]{:S(2)}, u32[]{:S(2)}) collective-permute-start(f32[2,2,8,128]{3,2,1,0:T(8,128)S(1)} %get-tuple-element.49), channel_id=1, source_target_pairs={{32,0},{64,32},{96,64},{128,96},{160,128},{192,160},{224,192},{33,... | collective-permute-start | bytes 49160 | tf_op jit(solution)/shard_map/ppermute | solution.py:31
  69.3 8.4 %collective-permute-start.6 = (f32[2,2,144,8]{3,2,1,0:T(8,128)S(1)}, f32[2,2,144,8]{3,2,1,0:T(8,128)S(1)}, u32[]{:S(2)}, u32[]{:S(2)}) collective-permute-start(f32[2,2,144,8]{3,2,1,0:T(8,128)S(1)} %get-tuple-element.38), channel_id=1, source_target_pairs={{0,1},{1,2},{2,3},{3,4},{4,5},{5,6},{6,7},{7,8},{8,9},{9,10},{10,1... | collective-permute-start | bytes 55304 | tf_op jit(solution)/shard_map/ppermute | solution.py:30
  72.4 10.2 %collective-permute-start.7 = (f32[2,2,144,8]{3,2,1,0:T(8,128)S(1)}, f32[2,2,144,8]{3,2,1,0:T(8,128)S(1)}, u32[]{:S(2)}, u32[]{:S(2)}) collective-permute-start(f32[2,2,144,8]{3,2,1,0:T(8,128)S(1)} %get-tuple-element.39), channel_id=1, source_target_pairs={{1,0},{2,1},{3,2},{4,3},{5,4},{6,5},{7,6},{8,7},{9,8},{10,9},{11,1... | collective-permute-start | bytes 55304 | tf_op jit(solution)/shard_map/ppermute | solution.py:31
  82.8 0.8 copy-start.3
  83.8 1.0 slice-start
  132.2 7.0 %collective-permute-start.8 = (f32[2,2,8,112]{3,2,1,0:T(8,128)S(1)}, f32[2,2,8,112]{3,2,1,0:T(8,128)S(1)}, u32[]{:S(2)}, u32[]{:S(2)}) collective-permute-start(f32[2,2,8,112]{3,2,1,0:T(8,128)S(1)} %get-tuple-element.58), channel_id=1, source_target_pairs={{0,32},{32,64},{64,96},{96,128},{128,160},{160,192},{192,224},{1,3... | collective-permute-start | bytes 43016 | tf_op jit(solution)/shard_map/ppermute | solution.py:30
  135.5 5.1 %collective-permute-start.9 = (f32[2,2,8,112]{3,2,1,0:T(8,128)S(1)}, f32[2,2,8,112]{3,2,1,0:T(8,128)S(1)}, u32[]{:S(2)}, u32[]{:S(2)}) collective-permute-start(f32[2,2,8,112]{3,2,1,0:T(8,128)S(1)} %get-tuple-element.59), channel_id=1, source_target_pairs={{32,0},{64,32},{96,64},{128,96},{160,128},{192,160},{224,192},{33,... | collective-permute-start | bytes 43016 | tf_op jit(solution)/shard_map/ppermute | solution.py:31
  140.7 8.2 %collective-permute-start.10 = (f32[2,2,128,8]{3,2,1,0:T(8,128)S(1)}, f32[2,2,128,8]{3,2,1,0:T(8,128)S(1)}, u32[]{:S(2)}, u32[]{:S(2)}) collective-permute-start(f32[2,2,128,8]{3,2,1,0:T(8,128)S(1)} %get-tuple-element.46), channel_id=1, source_target_pairs={{0,1},{1,2},{2,3},{3,4},{4,5},{5,6},{6,7},{7,8},{8,9},{9,10},{10,1... | collective-permute-start | bytes 49160 | tf_op jit(solution)/shard_map/ppermute | solution.py:30
  144.3 8.7 %collective-permute-start.11 = (f32[2,2,128,8]{3,2,1,0:T(8,128)S(1)}, f32[2,2,128,8]{3,2,1,0:T(8,128)S(1)}, u32[]{:S(2)}, u32[]{:S(2)}) collective-permute-start(f32[2,2,128,8]{3,2,1,0:T(8,128)S(1)} %get-tuple-element.47), channel_id=1, source_target_pairs={{1,0},{2,1},{3,2},{4,3},{5,4},{6,5},{7,6},{8,7},{9,8},{10,9},{11,1... | collective-permute-start | bytes 49160 | tf_op jit(solution)/shard_map/ppermute | solution.py:31
  155.8 4.6 %collective-permute-start.12 = (f32[2,2,8,128]{3,2,1,0:T(8,128)S(1)}, f32[2,2,8,128]{3,2,1,0:T(8,128)S(1)}, u32[]{:S(2)}, u32[]{:S(2)}) collective-permute-start(f32[2,2,8,128]{3,2,1,0:T(8,128)S(1)} %get-tuple-element.40), channel_id=1, source_target_pairs={{0,32},{32,64},{64,96},{96,128},{128,160},{160,192},{192,224},{1,3... | collective-permute-start | bytes 49160 | tf_op jit(solution)/shard_map/ppermute | solution.py:30
  158.3 5.1 %collective-permute-start.13 = (f32[2,2,8,128]{3,2,1,0:T(8,128)S(1)}, f32[2,2,8,128]{3,2,1,0:T(8,128)S(1)}, u32[]{:S(2)}, u32[]{:S(2)}) collective-permute-start(f32[2,2,8,128]{3,2,1,0:T(8,128)S(1)} %get-tuple-element.41), channel_id=1, source_target_pairs={{32,0},{64,32},{96,64},{128,96},{160,128},{192,160},{224,192},{33,... | collective-permute-start | bytes 49160 | tf_op jit(solution)/shard_map/ppermute | solution.py:31
  163.5 8.4 %collective-permute-start.14 = (f32[2,2,144,8]{3,2,1,0:T(8,128)S(1)}, f32[2,2,144,8]{3,2,1,0:T(8,128)S(1)}, u32[]{:S(2)}, u32[]{:S(2)}) collective-permute-start(f32[2,2,144,8]{3,2,1,0:T(8,128)S(1)} %get-tuple-element.36), channel_id=1, source_target_pairs={{0,1},{1,2},{2,3},{3,4},{4,5},{5,6},{6,7},{7,8},{8,9},{9,10},{10,1... | collective-permute-start | bytes 55304 | tf_op jit(solution)/shard_map/ppermute | solution.py:30
  166.7 10.5 %collective-permute-start.15 = (f32[2,2,144,8]{3,2,1,0:T(8,128)S(1)}, f32[2,2,144,8]{3,2,1,0:T(8,128)S(1)}, u32[]{:S(2)}, u32[]{:S(2)}) collective-permute-start(f32[2,2,144,8]{3,2,1,0:T(8,128)S(1)} %get-tuple-element.37), channel_id=1, source_target_pairs={{1,0},{2,1},{3,2},{4,3},{5,4},{6,5},{7,6},{8,7},{9,8},{10,9},{11,1... | collective-permute-start | bytes 55304 | tf_op jit(solution)/shard_map/ppermute | solution.py:31
  177.5 0.8 copy-start.4
  178.4 1.0 slice-start.1
